TPU v7x, 32 devices: a whole 2x2x4 slice. The times are simulated.
32 devices in a mesh: rows: 8 (over z, y), cols: 4 (over x, core).
Axes of the slice: x: 2, y: 2, z: 4, core: 2. Of those that a mesh axis runs over, the one named last changes fastest.
Arguments:
- sketches: bfloat16 [2048, 16384], P('rows', 'cols'), may hold values from -6 to 6, as said below
- start_basis: bfloat16 [16384, 256], P('cols'), may hold values from -6 to 6
- shrink_index: int32 [1], replicated, may hold values from 64 to 191
Outputs:
- shrunk: float32 [256, 16384], P('rows', 'cols')
Inputs may be any that keep to these rules, and one draw needn't show every extreme that they name: `sketches`: real entries.
All inputs are finite; a program needn't handle non-finite values.
Results may differ from a plain program's by a relative error of at most 0.0028.
Values may be sent and summed in bfloat16 or wider, within the bound.
A program may use at most 64 MiB of HBM per device.

v0:
```python
import jax
import jax.numpy as jnp
from jax import lax
from jax.sharding import PartitionSpec as P

ITERS = 3


def project(sketches, basis_bf):
    partial_product = jnp.dot(sketches, basis_bf, preferred_element_type=jnp.float32)
    return lax.psum(partial_product, "cols")


def orthonormal(images, gram_total):
    lower_factor = jnp.linalg.cholesky(gram_total)
    return jax.scipy.linalg.solve_triangular(lower_factor, images.T, lower=True).T


def body(sketches, start_basis, shrink_index):
    basis_bf = start_basis
    basis = start_basis.astype(jnp.float32)
    for loop_index in range(ITERS):
        projected_bf = project(sketches, basis_bf).astype(jnp.bfloat16)
        local_images = jnp.einsum(
            "lw,lk->wk", sketches, projected_bf, preferred_element_type=jnp.float32
        )
        images = lax.psum(local_images, "rows")
        gram_total = lax.psum(jnp.dot(images.T, images, precision=lax.Precision.HIGHEST), "cols")
        basis = orthonormal(images, gram_total)
        basis_bf = basis.astype(jnp.bfloat16)
    projected = project(sketches, basis_bf)
    energy = lax.psum(jnp.sum(projected * projected, axis=0), "rows")
    ordered = jnp.sort(energy)[::-1]
    threshold = lax.dynamic_index_in_dim(ordered, shrink_index[0], 0, keepdims=False)
    factor = jnp.sqrt(jnp.maximum(energy - threshold, 0.25 * threshold))
    owned_rows = basis.shape[1] // lax.axis_size("rows")
    offset = lax.axis_index("rows") * owned_rows
    columns = lax.dynamic_slice_in_dim(basis, offset, owned_rows, 1)
    scaled = columns * lax.dynamic_slice_in_dim(factor, offset, owned_rows, 0)[None, :]
    return scaled.T


def solution(mesh):
    return jax.shard_map(
        body,
        mesh=mesh,
        in_specs=(P("rows", "cols"), P("cols", None), P()),
        out_specs=P("rows", "cols"),
        check_vma=False,
    )
```

profile of v0, /device:TPU:0, one launch (start us, length us, event | category | flops | bytes accessed | tf_op | source)
XLA Modules:
  0.0 932.8 jit_solution(5308531713813557644)
XLA Ops:
  6.5 1.6 copy-done
  8.1 2.3 fusion.53
  10.4 16.3 %all-reduce.25 = bf16[256,256]{1,0:T(8,128)(2,1)S(1)} all-reduce(f32[256,256]{1,0:T(8,128)S(1)} %fusion.53), channel_id=1, replica_groups=mesh['rows'=8,'cols'=4] {'cols'}, use_global_device_ids=true, to_apply=%region_0.0 | all-reduce | flops 65536 | bytes 393216 | tf_op jit(solution)/shard_map/psum | solution.py:11
  26.7 2.7 convolution_bitcast_fusion.2
  29.5 157.0 %all-reduce.12.cloned.1.call-done = f32[4096,256]{0,1:T(8,128)} async-done(((f32[4096,256]{0,1:T(8,128)}), f32[4096,256]{0,1:T(8,128)}) %all-reduce.12.cloned.1.call-update) | async-done | bytes 4194320 | tf_op jit(solution)/shard_map/psum | solution.py:27
  186.5 7.7 fusion.54
  194.7 30.9 %all-reduce.14.cloned.1.call-done = f32[256,256]{0,1:T(8,128)} async-done(((f32[256,256]{0,1:T(8,128)}), f32[256,256]{0,1:T(8,128)}) %all-reduce.14.cloned.1.call-update) | async-done | bytes 262160 | tf_op jit(solution)/shard_map/psum | solution.py:28
  225.6 1.1 copy.5
  226.7 1.0 fusion.20
  227.7 11.7 %cholesky.172 = f32[128,128]{1,0:T(8,128)S(1)} custom-call(f32[128,128]{1,0:T(8,128)S(1)} %cholesky.270), custom_call_target="Cholesky" | custom-call | tf_op jit(solution)/shard_map/jit(cholesky)/cholesky | solution.py:15
  239.5 9.8 %custom-call.15 = f32[1,128,128]{1,2,0:T(8,128)S(1)} custom-call(f32[1,128,128]{2,1,0:T(8,128)S(1)} %get-tuple-element.74), custom_call_target="InvertDiagBlocksLowerTriangular" | custom-call | tf_op jit(solution)/shard_map/jit(cholesky)/cholesky | solution.py:15
  249.8 11.7 %cholesky.189 = f32[128,128]{1,0:T(8,128)S(1)} custom-call(f32[128,128]{1,0:T(8,128)S(1)} %convolution_subtract_fusion.5), custom_call_target="Cholesky" | custom-call | tf_op jit(solution)/shard_map/jit(cholesky)/cholesky | solution.py:15
  261.5 0.7 compare_reduce_fusion.4
  263.6 4.1 while.6
  264.4 1.4 bitcast_dynamic-update-slice_fusion.6
  266.3 1.4 bitcast_dynamic-update-slice_fusion.6
  267.7 19.7 %custom-call.16 = f32[2,128,128]{1,2,0:T(8,128)S(1)} custom-call(f32[2,128,128]{2,1,0:T(8,128)S(1)} %get-tuple-element.30), custom_call_target="InvertDiagBlocksLowerTriangular" | custom-call | tf_op jit(solution)/shard_map/jit(_solve_triangular)/triangular_solve | solution.py:16
  287.4 3.6 fusion.9
  291.1 2.0 convolution_subtract_fusion.2
  293.1 1.9 fusion.33
  295.0 0.9 fusion.14
  295.9 13.5 %all-reduce.26 = bf16[256,256]{0,1:T(8,128)(2,1)S(1)} all-reduce(f32[256,256]{0,1:T(8,128)S(1)} %fusion.14), channel_id=1, replica_groups=mesh['rows'=8,'cols'=4] {'cols'}, use_global_device_ids=true, to_apply=%region_7.0 | all-reduce | flops 65536 | bytes 393216 | tf_op jit(solution)/shard_map/psum | solution.py:11
  309.4 2.7 convolution_bitcast_fusion.1
  312.1 156.6 %all-reduce.16.cloned.1.call-done = f32[4096,256]{0,1:T(8,128)} async-done(((f32[4096,256]{0,1:T(8,128)}), f32[4096,256]{0,1:T(8,128)}) %all-reduce.16.cloned.1.call-update) | async-done | bytes 4194320 | tf_op jit(solution)/shard_map/psum | solution.py:27
  468.7 7.7 fusion.55
  476.9 31.0 %all-reduce.18.cloned.1.call-done = f32[256,256]{0,1:T(8,128)} async-done(((f32[256,256]{0,1:T(8,128)}), f32[256,256]{0,1:T(8,128)}) %all-reduce.18.cloned.1.call-update) | async-done | bytes 262160 | tf_op jit(solution)/shard_map/psum | solution.py:28
  507.9 1.1 copy.7
  508.9 1.0 fusion.19
  509.9 11.7 %cholesky.206 = f32[128,128]{1,0:T(8,128)S(1)} custom-call(f32[128,128]{1,0:T(8,128)S(1)} %cholesky.273), custom_call_target="Cholesky" | custom-call | tf_op jit(solution)/shard_map/jit(cholesky)/cholesky | solution.py:15
  521.7 9.8 %custom-call.17 = f32[1,128,128]{1,2,0:T(8,128)S(1)} custom-call(f32[1,128,128]{2,1,0:T(8,128)S(1)} %get-tuple-element.70), custom_call_target="InvertDiagBlocksLowerTriangular" | custom-call | tf_op jit(solution)/shard_map/jit(cholesky)/cholesky | solution.py:15
  532.0 11.7 %cholesky.223 = f32[128,128]{1,0:T(8,128)S(1)} custom-call(f32[128,128]{1,0:T(8,128)S(1)} %convolution_subtract_fusion.4), custom_call_target="Cholesky" | custom-call | tf_op jit(solution)/shard_map/jit(cholesky)/cholesky | solution.py:15
  546.4 4.1 while.7
  547.2 1.4 bitcast_dynamic-update-slice_fusion.7
  549.1 1.4 bitcast_dynamic-update-slice_fusion.7
  550.5 19.7 %custom-call.18 = f32[2,128,128]{1,2,0:T(8,128)S(1)} custom-call(f32[2,128,128]{2,1,0:T(8,128)S(1)} %get-tuple-element.31), custom_call_target="InvertDiagBlocksLowerTriangular" | custom-call | tf_op jit(solution)/shard_map/jit(_solve_triangular)/triangular_solve | solution.py:16
  570.2 3.6 fusion.7
  573.8 2.0 convolution_subtract_fusion.1
  575.8 1.9 fusion.29
  577.8 0.9 fusion.15
  578.7 13.5 %all-reduce.27 = bf16[256,256]{0,1:T(8,128)(2,1)S(1)} all-reduce(f32[256,256]{0,1:T(8,128)S(1)} %fusion.15), channel_id=1, replica_groups=mesh['rows'=8,'cols'=4] {'cols'}, use_global_device_ids=true, to_apply=%region_10.0 | all-reduce | flops 65536 | bytes 393216 | tf_op jit(solution)/shard_map/psum | solution.py:11
  592.2 2.7 convolution_bitcast_fusion
  594.9 156.5 %all-reduce.20.cloned.1.call-done = f32[4096,256]{0,1:T(8,128)} async-done(((f32[4096,256]{0,1:T(8,128)}), f32[4096,256]{0,1:T(8,128)}) %all-reduce.20.cloned.1.call-update) | async-done | bytes 4194320 | tf_op jit(solution)/shard_map/psum | solution.py:27
  751.5 7.7 fusion.56
  759.4 31.2 %all-reduce.22.cloned.1.call-done = f32[256,256]{0,1:T(8,128)} async-done(((f32[256,256]{0,1:T(8,128)}), f32[256,256]{0,1:T(8,128)}) %all-reduce.22.cloned.1.call-update) | async-done | bytes 262160 | tf_op jit(solution)/shard_map/psum | solution.py:28
  790.6 1.1 copy.9
  791.7 1.0 fusion.18
  792.7 11.7 %cholesky.240 = f32[128,128]{1,0:T(8,128)S(1)} custom-call(f32[128,128]{1,0:T(8,128)S(1)} %cholesky.276), custom_call_target="Cholesky" | custom-call | tf_op jit(solution)/shard_map/jit(cholesky)/cholesky | solution.py:15
  804.5 9.8 %custom-call.19 = f32[1,128,128]{1,2,0:T(8,128)S(1)} custom-call(f32[1,128,128]{2,1,0:T(8,128)S(1)} %get-tuple-element.66), custom_call_target="InvertDiagBlocksLowerTriangular" | custom-call | tf_op jit(solution)/shard_map/jit(cholesky)/cholesky | solution.py:15
  814.8 11.7 %cholesky.257 = f32[128,128]{1,0:T(8,128)S(1)} custom-call(f32[128,128]{1,0:T(8,128)S(1)} %convolution_subtract_fusion.3), custom_call_target="Cholesky" | custom-call | tf_op jit(solution)/shard_map/jit(cholesky)/cholesky | solution.py:15
  829.1 4.2 while.8
  830.0 1.4 bitcast_dynamic-update-slice_fusion.8
  832.0 1.4 bitcast_dynamic-update-slice_fusion.8
  833.3 19.7 %custom-call.20 = f32[2,128,128]{1,2,0:T(8,128)S(1)} custom-call(f32[2,128,128]{2,1,0:T(8,128)S(1)} %get-tuple-element.32), custom_call_target="InvertDiagBlocksLowerTriangular" | custom-call | tf_op jit(solution)/shard_map/jit(_solve_triangular)/triangular_solve | solution.py:16
  853.0 3.6 fusion.5
  856.7 1.9 convolution_subtract_fusion
  858.6 1.9 fusion.25
  860.6 1.3 copy-done.5
  861.9 1.5 fusion.11
  864.0 31.8 %all-reduce.24.cloned.1.call-done = f32[256,256]{0,1:T(8,128)} async-done(((f32[256,256]{0,1:T(8,128)}), f32[256,256]{0,1:T(8,128)}) %all-reduce.24.cloned.1.call-update) | async-done | bytes 262160 | tf_op jit(solution)/shard_map/psum | solution.py:11
  895.8 1.1 multiply_reduce_fusion
  896.9 21.4 %psum.87 = f32[256]{0:T(256)S(1)} all-reduce(f32[256]{0:T(256)S(1)} %multiply_reduce_fusion), channel_id=1, replica_groups=mesh['rows'=8,'cols'=4] {'rows'}, use_global_device_ids=true, to_apply=%region_15.18 | all-reduce | flops 256 | bytes 2048 | tf_op jit(solution)/shard_map/psum | solution.py:32
  918.3 3.3 sort.15
  922.9 0.7 maximum_sqrt_fusion
  923.6 1.9 fusion.17
  (70 shorter events, 10.2 us)
Async XLA Ops:
  6.5 1.6 copy-start
  6.5 179.9 %all-reduce.12.cloned.1.call-start = ((), (), s32[]{:S(2)}) async-start(), calls=%async_computation | async-start | bytes 8388608 | tf_op jit(solution)/shard_map/psum | solution.py:27
  29.4 196.2 %all-reduce.14.cloned.1.call-start = ((), (), s32[]{:S(2)}) async-start(), calls=%async_computation.1 | async-start | bytes 524288 | tf_op jit(solution)/shard_map/psum | solution.py:28
  194.2 274.5 %all-reduce.16.cloned.1.call-start = ((), (), s32[]{:S(2)}) async-start(), calls=%async_computation.2 | async-start | bytes 8388608 | tf_op jit(solution)/shard_map/psum | solution.py:27
  287.4 3.7 copy-start.1
  312.1 195.8 %all-reduce.18.cloned.1.call-start = ((), (), s32[]{:S(2)}) async-start(), calls=%async_computation.3 | async-start | bytes 524288 | tf_op jit(solution)/shard_map/psum | solution.py:28
  476.4 275.0 %all-reduce.20.cloned.1.call-start = ((), (), s32[]{:S(2)}) async-start(), calls=%async_computation.4 | async-start | bytes 8388608 | tf_op jit(solution)/shard_map/psum | solution.py:27
  570.2 3.7 copy-start.3
  594.9 195.7 %all-reduce.22.cloned.1.call-start = ((), (), s32[]{:S(2)}) async-start(), calls=%async_computation.5 | async-start | bytes 524288 | tf_op jit(solution)/shard_map/psum | solution.py:28
  759.2 136.6 %all-reduce.24.cloned.1.call-start = ((), (), s32[]{:S(2)}) async-start(), calls=%async_computation.6 | async-start | bytes 524288 | tf_op jit(solution)/shard_map/psum | solution.py:11
  853.0 3.7 copy-start.2
  856.7 3.9 copy-start.4
  860.6 1.3 copy-start.5
Sparse Core Ops, SparseCore 0:
  29.6 156.8 all-reduce.11
  194.3 31.2 all-reduce.13
  312.2 156.4 all-reduce.15
  476.5 31.2 all-reduce.17
  595.0 156.4 all-reduce.19
  759.3 31.2 all-reduce.21
  863.5 32.2 all-reduce.23
where the time goes:
time: 938 us; the launch traced here: 933 us
  waiting for transfers between devices  595 us (63%)
  other arithmetic  172 us (18%)
  blocking collectives  64.6 us (7%)
  matrix products  60.7 us (6%)
  between operations  19.5 us (2%)
  local copies, waits for them, and re-layouts  18.7 us (2%)
    psum x3, waiting for transfers between devices, body(): images = lax.psum(local_images, 'rows')  470 us
    another operation x20, other arithmetic, orthonormal(): lower_factor = jnp.linalg.cholesky(gram_total)  103 us
    psum x3, waiting for transfers between devices, body(): lax.psum(jnp.dot(images.T, images, precision=lax.Precision.HIGHEST), 'cols')  93 us
    another operation x7, other arithmetic, orthonormal(): jax.scipy.linalg.solve_triangular(lower_factor, images.T, lower=True)  59.1 us
    psum x3, blocking collectives, project(): return lax.psum(partial_product, 'cols')  43.3 us
    psum x1, waiting for transfers between devices, project(): return lax.psum(partial_product, 'cols')  31.8 us
    dot_general x3, matrix products, body(): jnp.dot(images.T, images, precision=lax.Precision.HIGHEST)  23.1 us
    another operation x9, matrix products, orthonormal(): jax.scipy.linalg.solve_triangular(lower_factor, images.T, lower=True)  22.6 us
  transfers between devices with their start and end apart: 7, of which 7 were waited for; matrix products, arithmetic and copies ran while one was open for 0% of the time, Pallas kernels for 0%

commit v1 on v0

--- a/solution.py
+++ b/solution.py
@@ -25,7 +25,10 @@
             "lw,lk->wk", sketches, projected_bf, preferred_element_type=jnp.float32
         )
         images = lax.psum(local_images, "rows")
-        gram_total = lax.psum(jnp.dot(images.T, images, precision=lax.Precision.HIGHEST), "cols")
+        gram_total = jnp.sum(
+            lax.all_gather(jnp.dot(images.T, images, precision=lax.Precision.HIGHEST), "cols"),
+            axis=0,
+        )
         basis = orthonormal(images, gram_total)
         basis_bf = basis.astype(jnp.bfloat16)
     projected = project(sketches, basis_bf)

time: 938 us -> 891 us (0.950)
  waiting for transfers between devices: 595 us -> 550 us
    psum x3 -> x0, waiting for transfers between devices: 93 us -> none  [body(): lax.psum(jnp.dot(images.T, images, precision=lax.Precision.HIGHEST), 'cols')]
    all_gather x0 -> x3, waiting for transfers between devices: none -> 46.3 us  [body(): lax.all_gather(jnp.dot(images.T, images, precision=lax.Precision.HIGHEST)...]
where the time goes in v1:
time: 891 us; the launch traced here: 886 us
  waiting for transfers between devices  550 us (62%)
  other arithmetic  173 us (19%)
  blocking collectives  64.9 us (7%)
  matrix products  60.7 us (7%)
  between operations  19.5 us (2%)
  local copies, waits for them, and re-layouts  15.9 us (2%)
    psum x3, waiting for transfers between devices, body(): images = lax.psum(local_images, 'rows')  472 us
    another operation x20, other arithmetic, orthonormal(): lower_factor = jnp.linalg.cholesky(gram_total)  103 us
    another operation x7, other arithmetic, orthonormal(): jax.scipy.linalg.solve_triangular(lower_factor, images.T, lower=True)  59.1 us
    all_gather x3, waiting for transfers between devices, body(): lax.all_gather(jnp.dot(images.T, images, precision=lax.Precision.HIGHEST)...  46.3 us
    psum x3, blocking collectives, project(): return lax.psum(partial_product, 'cols')  43.5 us
    psum x1, waiting for transfers between devices, project(): return lax.psum(partial_product, 'cols')  31.8 us
    dot_general x3, matrix products, body(): jnp.dot(images.T, images, precision=lax.Precision.HIGHEST)  23.1 us
    another operation x9, matrix products, orthonormal(): jax.scipy.linalg.solve_triangular(lower_factor, images.T, lower=True)  22.6 us
  transfers between devices with their start and end apart: 7, of which 7 were waited for; matrix products, arithmetic and copies ran while one was open for 0% of the time, Pallas kernels for 0%

profile of v1, /device:TPU:0, one launch (start us, length us, event | category | flops | bytes accessed | tf_op | source)
XLA Modules:
  0.0 886.2 jit_solution(11373086289368153035)
XLA Ops:
  6.5 1.6 copy-done
  8.1 2.3 fusion.53
  10.4 16.3 %all-reduce.16 = bf16[256,256]{1,0:T(8,128)(2,1)S(1)} all-reduce(f32[256,256]{1,0:T(8,128)S(1)} %fusion.53), channel_id=1, replica_groups=mesh['rows'=8,'cols'=4] {'cols'}, use_global_device_ids=true, to_apply=%region_0.0 | all-reduce | flops 65536 | bytes 393216 | tf_op jit(solution)/shard_map/psum | solution.py:11
  26.7 2.7 convolution_bitcast_fusion.2
  29.5 157.0 %all-reduce.9.cloned.1.call-done = f32[4096,256]{0,1:T(8,128)} async-done(((f32[4096,256]{0,1:T(8,128)}), f32[4096,256]{0,1:T(8,128)}) %all-reduce.9.cloned.1.call-update) | async-done | bytes 4194320 | tf_op jit(solution)/shard_map/psum | solution.py:27
  186.5 7.7 fusion.54
  194.7 15.3 %all-gather.7.cloned.1.call-done = f32[1024,256]{1,0:T(8,128)} async-done(((f32[256,256]{1,0:T(8,128)}), f32[1024,256]{1,0:T(8,128)}) %all-gather.7.cloned.1.call-update) | async-done | bytes 1048592 | tf_op jit(solution)/shard_map/all_gather | solution.py:29
  210.0 1.3 reduce_sum.36
  211.6 11.7 %cholesky.172 = f32[128,128]{1,0:T(8,128)S(1)} custom-call(f32[128,128]{1,0:T(8,128)S(1)} %cholesky.270), custom_call_target="Cholesky" | custom-call | tf_op jit(solution)/shard_map/jit(cholesky)/cholesky | solution.py:15
  223.3 9.8 %custom-call.15 = f32[1,128,128]{1,2,0:T(8,128)S(1)} custom-call(f32[1,128,128]{2,1,0:T(8,128)S(1)} %get-tuple-element.74), custom_call_target="InvertDiagBlocksLowerTriangular" | custom-call | tf_op jit(solution)/shard_map/jit(cholesky)/cholesky | solution.py:15
  233.6 11.7 %cholesky.189 = f32[128,128]{1,0:T(8,128)S(1)} custom-call(f32[128,128]{1,0:T(8,128)S(1)} %convolution_subtract_fusion.5), custom_call_target="Cholesky" | custom-call | tf_op jit(solution)/shard_map/jit(cholesky)/cholesky | solution.py:15
  245.4 0.7 compare_reduce_fusion.4
  247.4 4.1 while.6
  248.2 1.4 bitcast_dynamic-update-slice_fusion.6
  250.2 1.4 bitcast_dynamic-update-slice_fusion.6
  251.6 19.7 %custom-call.16 = f32[2,128,128]{1,2,0:T(8,128)S(1)} custom-call(f32[2,128,128]{2,1,0:T(8,128)S(1)} %get-tuple-element.30), custom_call_target="InvertDiagBlocksLowerTriangular" | custom-call | tf_op jit(solution)/shard_map/jit(_solve_triangular)/triangular_solve | solution.py:16
  271.3 3.6 fusion.9
  274.9 2.0 convolution_subtract_fusion.2
  276.9 1.9 fusion.33
  278.8 0.9 fusion.14
  279.7 13.6 %all-reduce.17 = bf16[256,256]{0,1:T(8,128)(2,1)S(1)} all-reduce(f32[256,256]{0,1:T(8,128)S(1)} %fusion.14), channel_id=1, replica_groups=mesh['rows'=8,'cols'=4] {'cols'}, use_global_device_ids=true, to_apply=%region_7.0 | all-reduce | flops 65536 | bytes 393216 | tf_op jit(solution)/shard_map/psum | solution.py:11
  293.4 2.7 convolution_bitcast_fusion.1
  296.1 157.4 %all-reduce.11.cloned.1.call-done = f32[4096,256]{0,1:T(8,128)} async-done(((f32[4096,256]{0,1:T(8,128)}), f32[4096,256]{0,1:T(8,128)}) %all-reduce.11.cloned.1.call-update) | async-done | bytes 4194320 | tf_op jit(solution)/shard_map/psum | solution.py:27
  453.5 7.7 fusion.55
  461.6 15.4 %all-gather.9.cloned.1.call-done = f32[1024,256]{1,0:T(8,128)} async-done(((f32[256,256]{1,0:T(8,128)}), f32[1024,256]{1,0:T(8,128)}) %all-gather.9.cloned.1.call-update) | async-done | bytes 1048592 | tf_op jit(solution)/shard_map/all_gather | solution.py:29
  477.0 1.3 reduce_sum.37
  478.6 11.7 %cholesky.206 = f32[128,128]{1,0:T(8,128)S(1)} custom-call(f32[128,128]{1,0:T(8,128)S(1)} %cholesky.273), custom_call_target="Cholesky" | custom-call | tf_op jit(solution)/shard_map/jit(cholesky)/cholesky | solution.py:15
  490.3 9.8 %custom-call.17 = f32[1,128,128]{1,2,0:T(8,128)S(1)} custom-call(f32[1,128,128]{2,1,0:T(8,128)S(1)} %get-tuple-element.70), custom_call_target="InvertDiagBlocksLowerTriangular" | custom-call | tf_op jit(solution)/shard_map/jit(cholesky)/cholesky | solution.py:15
  500.6 11.7 %cholesky.223 = f32[128,128]{1,0:T(8,128)S(1)} custom-call(f32[128,128]{1,0:T(8,128)S(1)} %convolution_subtract_fusion.4), custom_call_target="Cholesky" | custom-call | tf_op jit(solution)/shard_map/jit(cholesky)/cholesky | solution.py:15
  512.4 0.6 compare_reduce_fusion.2
  513.0 0.6 compare_reduce_fusion.3
  515.0 4.1 while.7
  515.8 1.4 bitcast_dynamic-update-slice_fusion.7
  517.7 1.4 bitcast_dynamic-update-slice_fusion.7
  519.1 19.7 %custom-call.18 = f32[2,128,128]{1,2,0:T(8,128)S(1)} custom-call(f32[2,128,128]{2,1,0:T(8,128)S(1)} %get-tuple-element.31), custom_call_target="InvertDiagBlocksLowerTriangular" | custom-call | tf_op jit(solution)/shard_map/jit(_solve_triangular)/triangular_solve | solution.py:16
  538.8 3.6 fusion.7
  542.5 2.0 convolution_subtract_fusion.1
  544.4 1.9 fusion.29
  546.4 0.9 fusion.15
  547.3 13.6 %all-reduce.18 = bf16[256,256]{0,1:T(8,128)(2,1)S(1)} all-reduce(f32[256,256]{0,1:T(8,128)S(1)} %fusion.15), channel_id=1, replica_groups=mesh['rows'=8,'cols'=4] {'cols'}, use_global_device_ids=true, to_apply=%region_10.0 | all-reduce | flops 65536 | bytes 393216 | tf_op jit(solution)/shard_map/psum | solution.py:11
  560.9 2.7 convolution_bitcast_fusion
  563.7 157.4 %all-reduce.13.cloned.1.call-done = f32[4096,256]{0,1:T(8,128)} async-done(((f32[4096,256]{0,1:T(8,128)}), f32[4096,256]{0,1:T(8,128)}) %all-reduce.13.cloned.1.call-update) | async-done | bytes 4194320 | tf_op jit(solution)/shard_map/psum | solution.py:27
  721.0 7.7 fusion.56
  729.0 15.6 %all-gather.11.cloned.1.call-done = f32[1024,256]{1,0:T(8,128)} async-done(((f32[256,256]{1,0:T(8,128)}), f32[1024,256]{1,0:T(8,128)}) %all-gather.11.cloned.1.call-update) | async-done | bytes 1048592 | tf_op jit(solution)/shard_map/all_gather | solution.py:29
  744.6 1.3 reduce_sum.38
  746.1 11.7 %cholesky.240 = f32[128,128]{1,0:T(8,128)S(1)} custom-call(f32[128,128]{1,0:T(8,128)S(1)} %cholesky.276), custom_call_target="Cholesky" | custom-call | tf_op jit(solution)/shard_map/jit(cholesky)/cholesky | solution.py:15
  757.9 9.8 %custom-call.19 = f32[1,128,128]{1,2,0:T(8,128)S(1)} custom-call(f32[1,128,128]{2,1,0:T(8,128)S(1)} %get-tuple-element.66), custom_call_target="InvertDiagBlocksLowerTriangular" | custom-call | tf_op jit(solution)/shard_map/jit(cholesky)/cholesky | solution.py:15
  768.2 11.7 %cholesky.257 = f32[128,128]{1,0:T(8,128)S(1)} custom-call(f32[128,128]{1,0:T(8,128)S(1)} %convolution_subtract_fusion.3), custom_call_target="Cholesky" | custom-call | tf_op jit(solution)/shard_map/jit(cholesky)/cholesky | solution.py:15
  779.9 0.6 compare_reduce_fusion
  782.5 4.2 while.8
  783.4 1.4 bitcast_dynamic-update-slice_fusion.8
  785.4 1.4 bitcast_dynamic-update-slice_fusion.8
  786.8 19.7 %custom-call.20 = f32[2,128,128]{1,2,0:T(8,128)S(1)} custom-call(f32[2,128,128]{2,1,0:T(8,128)S(1)} %get-tuple-element.32), custom_call_target="InvertDiagBlocksLowerTriangular" | custom-call | tf_op jit(solution)/shard_map/jit(_solve_triangular)/triangular_solve | solution.py:16
  806.4 3.6 fusion.5
  810.1 1.9 convolution_subtract_fusion
  812.0 1.9 fusion.25
  814.0 1.3 copy-done.5
  815.3 1.5 fusion.11
  817.5 31.8 %all-reduce.15.cloned.1.call-done = f32[256,256]{0,1:T(8,128)} async-done(((f32[256,256]{0,1:T(8,128)}), f32[256,256]{0,1:T(8,128)}) %all-reduce.15.cloned.1.call-update) | async-done | bytes 262160 | tf_op jit(solution)/shard_map/psum | solution.py:11
  849.3 1.1 multiply_reduce_fusion
  850.3 21.4 %psum.63 = f32[256]{0:T(256)S(1)} all-reduce(f32[256]{0:T(256)S(1)} %multiply_reduce_fusion), channel_id=1, replica_groups=mesh['rows'=8,'cols'=4] {'rows'}, use_global_device_ids=true, to_apply=%region_15.18 | all-reduce | flops 256 | bytes 2048 | tf_op jit(solution)/shard_map/psum | solution.py:35
  871.7 3.3 sort.15
  876.3 0.7 maximum_sqrt_fusion
  877.0 1.9 fusion.17
  (73 shorter events, 8.8 us)
Async XLA Ops:
  6.5 1.6 copy-start
  6.5 179.9 %all-reduce.9.cloned.1.call-start = ((), (), s32[]{:S(2)}) async-start(), calls=%async_computation | async-start | bytes 8388608 | tf_op jit(solution)/shard_map/psum | solution.py:27
  29.4 180.6 %all-gather.7.cloned.1.call-start = ((), (), s32[]{:S(2)}) async-start(), calls=%async_computation.4 | async-start | bytes 1310720 | tf_op jit(solution)/shard_map/all_gather | solution.py:29
  194.2 259.3 %all-reduce.11.cloned.1.call-start = ((), (), s32[]{:S(2)}) async-start(), calls=%async_computation.1 | async-start | bytes 8388608 | tf_op jit(solution)/shard_map/psum | solution.py:27
  271.2 3.7 copy-start.1
  296.1 181.0 %all-gather.9.cloned.1.call-start = ((), (), s32[]{:S(2)}) async-start(), calls=%async_computation.5 | async-start | bytes 1310720 | tf_op jit(solution)/shard_map/all_gather | solution.py:29
  461.2 259.9 %all-reduce.13.cloned.1.call-start = ((), (), s32[]{:S(2)}) async-start(), calls=%async_computation.2 | async-start | bytes 8388608 | tf_op jit(solution)/shard_map/psum | solution.py:27
  538.8 3.7 copy-start.3
  563.6 181.0 %all-gather.11.cloned.1.call-start = ((), (), s32[]{:S(2)}) async-start(), calls=%async_computation.6 | async-start | bytes 1310720 | tf_op jit(solution)/shard_map/all_gather | solution.py:29
  728.8 120.5 %all-reduce.15.cloned.1.call-start = ((), (), s32[]{:S(2)}) async-start(), calls=%async_computation.3 | async-start | bytes 524288 | tf_op jit(solution)/shard_map/psum | solution.py:11
  806.4 3.7 copy-start.2
  810.1 3.9 copy-start.4
  814.0 1.3 copy-start.5
Sparse Core Ops, SparseCore 0:
  29.6 156.8 all-reduce.8
  194.3 15.6 all-gather.6
  296.2 157.2 all-reduce.10
  461.3 15.6 all-gather.8
  563.7 157.2 all-reduce.12
  728.9 15.6 all-gather.10
  816.9 32.2 all-reduce.14
